TPU v7x, 256 devices: a whole 4x4x8 slice. The times are simulated.
256 devices in a mesh: gx: 8 (over y, core), gy: 32 (over x, z).
Axes of the slice: x: 4, y: 4, z: 8, core: 2. Of those that a mesh axis runs over, the one named last changes fastest.
Arguments:
- right_side: float32 [64, 512, 256], P('gx', 'gy'), may hold values from -8 to 8
- velocity: float32 [3, 64, 512, 256], P(None, 'gx', 'gy'), may hold values from 0.1 to 3
- deflation: bfloat16 [32, 64, 512, 256], P(None, 'gx', 'gy'), may hold values from -0.1875 to 0.1875
- inverse_rows: float32 [8192, 8192], P(('gx', 'gy')), may hold values from -0.0625 to 0.0625
Outputs:
- solution_field: float32 [64, 512, 256], P('gx', 'gy')
- residual: float32 [64, 512, 256], P('gx', 'gy')
All inputs are finite; a program needn't handle non-finite values.
Results may differ from a plain program's by a relative error of at most 0.005.
Values sent between devices are 32-bit elements; how exact they have to be, the bound alone decides.
A program may use at most 64 MiB of HBM per device.

v0:
```python
import jax
import jax.numpy as jnp
from jax import lax
from jax.sharding import PartitionSpec as P

KD = 32
DEPTH = 2
CHEB = 4
cheb_center = 1.0
cheb_radius = 0.9


def with_halo(block, sides, width):
    for axis, dim in sides:
        count = lax.axis_size(axis)
        forward = [(i, i + 1) for i in range(count - 1)]
        backward = [(target, source) for source, target in forward]
        low = lax.ppermute(
            lax.slice_in_dim(block, block.shape[dim] - width, None, axis=dim), axis, forward
        )
        high = lax.ppermute(lax.slice_in_dim(block, 0, width, axis=dim), axis, backward)
        block = jnp.concatenate([low, block, high], axis=dim)
    return block


def upwind(padded, velocity):
    centre = padded[1:-1, 1:-1, 1:-1]
    diagonal = 6.0 + velocity[0] + velocity[1] + velocity[2]
    beside = padded[2:, 1:-1, 1:-1] + (1.0 + velocity[0]) * padded[:-2, 1:-1, 1:-1]
    beside = beside + padded[1:-1, 2:, 1:-1] + (1.0 + velocity[1]) * padded[1:-1, :-2, 1:-1]
    beside = beside + padded[1:-1, 1:-1, 2:] + (1.0 + velocity[2]) * padded[1:-1, 1:-1, :-2]
    return diagonal * centre - beside


def box_apply(field, velocity):
    return upwind(jnp.pad(field, 1), velocity)


def chebyshev(source, velocity, inside):
    inverse_diag = 1.0 / (6.0 + velocity[0] + velocity[1] + velocity[2])
    sigma_ratio = cheb_center / cheb_radius
    rho_now = 1.0 / sigma_ratio
    update = inverse_diag * source / cheb_center * inside
    estimate = update
    remainder = source
    for sweep_index in range(CHEB - 1):
        remainder = remainder - box_apply(update, velocity)
        rho_next = 1.0 / (2.0 * sigma_ratio - rho_now)
        update = (
            rho_next * rho_now * update + 2.0 * rho_next / cheb_radius * inverse_diag * remainder
        ) * inside
        estimate = estimate + update
        rho_now = rho_next
    return estimate


def apply_global(field, velocity):
    padded = with_halo(field, (("gx", 0), ("gy", 1)), 1)
    padded = jnp.pad(padded, ((0, 0), (0, 0), (1, 1)))
    return upwind(padded, velocity)


def precondition(residual, velocity, wide_velocity, flat_vectors, inverse_rows, inside):
    size_x, size_y, size_z = residual.shape
    coarse = jnp.dot(
        flat_vectors, residual.astype(jnp.bfloat16).reshape(-1), preferred_element_type=jnp.float32
    )
    gathered = lax.all_gather(coarse, ("gx", "gy"), axis=0, tiled=True)
    solved = jnp.dot(inverse_rows, gathered, precision=lax.Precision.HIGHEST)
    solved = solved.astype(jnp.bfloat16)
    correction = jnp.dot(solved, flat_vectors, preferred_element_type=jnp.float32).reshape(
        size_x, size_y, size_z
    )
    remaining = residual - apply_global(correction, velocity)
    source = with_halo(remaining, (("gx", 0), ("gy", 1)), DEPTH)
    estimate = chebyshev(source, wide_velocity, inside)
    return correction + estimate[DEPTH : DEPTH + size_x, DEPTH : DEPTH + size_y]


def local(right_side, velocity, deflation, inverse_rows):
    size_x, size_y, size_z = right_side.shape
    wide_velocity = with_halo(velocity, (("gx", 1), ("gy", 2)), DEPTH)
    rows_x = lax.axis_index("gx") * size_x - DEPTH + lax.iota(jnp.int32, size_x + 2 * DEPTH)
    rows_y = lax.axis_index("gy") * size_y - DEPTH + lax.iota(jnp.int32, size_y + 2 * DEPTH)
    inside_x = ((rows_x >= 0) & (rows_x < size_x * lax.axis_size("gx"))).astype(jnp.float32)
    inside_y = ((rows_y >= 0) & (rows_y < size_y * lax.axis_size("gy"))).astype(jnp.float32)
    inside = inside_x[:, None, None] * inside_y[None, :, None]
    flat_vectors = deflation.reshape(KD, -1)
    rho_now = lax.psum(jnp.sum(right_side * right_side), ("gx", "gy"))
    search = precondition(right_side, velocity, wide_velocity, flat_vectors, inverse_rows, inside)
    image = apply_global(search, velocity)
    denominator = lax.psum(jnp.sum(right_side * image), ("gx", "gy"))
    alpha_step = rho_now / denominator
    middle = right_side - alpha_step * image
    smoothed = precondition(middle, velocity, wide_velocity, flat_vectors, inverse_rows, inside)
    turned = apply_global(smoothed, velocity)
    cross, square = lax.psum((jnp.sum(turned * middle), jnp.sum(turned * turned)), ("gx", "gy"))
    omega_step = cross / square
    solution_field = alpha_step * search + omega_step * smoothed
    return (solution_field, middle - omega_step * turned)


def solution(mesh):
    return jax.shard_map(
        local,
        mesh=mesh,
        in_specs=(
            P("gx", "gy", None),
            P(None, "gx", "gy", None),
            P(None, "gx", "gy", None),
            P(("gx", "gy"), None),
        ),
        out_specs=(P("gx", "gy", None), P("gx", "gy", None)),
        check_vma=False,
    )
```

profile of v0, /device:TPU:1, one launch (start us, length us, event | category | flops | bytes accessed | tf_op | source)
XLA Modules:
  0.0 445.5 jit_solution(6390966304339603937)
XLA Ops:
  0.7 1.1 convert_bitcast_fusion.1
  1.7 2.8 fusion.8
  4.8 81.3 %all-reduce.10 = f32[8192]{0:T(1024)} all-reduce(f32[8192]{0:T(1024)S(1)} %dynamic-update-slice), channel_id=1, replica_groups=mesh['gx'=8,'gy'=32] {'gx','gy'}, use_global_device_ids=true, to_apply=%add.10 | all-reduce | flops 8192 | bytes 65536
  86.1 1.2 copy.11
  87.3 0.9 fusion.5
  88.3 0.4 copy-done.1
  88.7 0.4 fusion.131
  89.1 1.9 collective-permute-start.5
  91.0 2.4 collective-permute-start.4
  93.5 3.2 collective-permute-start
  96.6 1.9 collective-permute-start.1
  98.7 1.3 collective-permute-start.6
  100.0 4.0 collective-permute-start.7
  104.2 0.6 collective-permute-done.7
  104.8 0.2 select_maximum_fusion.10
  105.2 4.8 %collective-permute-start.8 = (f32[2,16,256]{2,1,0:T(8,128)S(1)}, f32[2,16,256]{2,1,0:T(8,128)S(1)}, u32[]{:S(2)}, u32[]{:S(2)}) collective-permute-start(f32[2,16,256]{2,1,0:T(8,128)S(1)} %get-tuple-element.52), channel_id=1, source_target_pairs={{0,32},{32,64},{64,96},{96,128},{128,160},{160,192},{192,224},{1,3... | collective-permute-start | bytes 98312 | tf_op jit(solution)/shard_map/ppermute | solution.py:18
  110.0 1.9 collective-permute-start.9
  112.1 3.9 collective-permute-start.2
  116.0 1.3 collective-permute-start.3
  117.4 4.0 collective-permute-start.10
  121.4 1.3 collective-permute-start.11
  122.9 3.0 collective-permute-done.11
  126.0 0.4 add_multiply_fusion.3
  126.5 0.4 bitcast_multiply_fusion.3
  126.9 0.3 fusion.39
  127.3 1.9 collective-permute-start.12
  129.3 5.6 %collective-permute-start.13 = (f32[1,16,256]{2,1,0:T(8,128)S(1)}, f32[1,16,256]{2,1,0:T(8,128)S(1)}, u32[]{:S(2)}, u32[]{:S(2)}) collective-permute-start(f32[1,16,256]{2,1,0:T(8,128)S(1)} %get-tuple-element.50), channel_id=1, source_target_pairs={{0,32},{32,64},{64,96},{96,128},{128,160},{160,192},{192,224},{1,3... | collective-permute-start | bytes 49160 | tf_op jit(solution)/shard_map/ppermute | solution.py:18
  134.9 0.8 collective-permute-done.13
  135.8 1.3 collective-permute-start.14
  137.1 4.0 collective-permute-start.15
  141.1 0.8 collective-permute-done.15
  142.1 0.8 multiply_reduce_fusion.2
  142.8 87.5 %all-reduce.13 = (f32[]{:T(128)}, f32[]{:T(128)}) all-reduce(f32[]{:T(128)} %get-tuple-element.5, f32[]{:T(128)} %get-tuple-element.4), channel_id=1, replica_groups=mesh['gx'=8,'gy'=32] {'gx','gy'}, use_global_device_ids=true, to_apply=%region_1.0 | all-reduce | flops 2 | bytes 16 | tf_op jit(solution)/shard_map/psum | solution.py:89
  231.8 3.0 fusion.11
  235.0 73.9 %all-reduce.11 = f32[8192]{0:T(1024)S(1)} all-reduce(f32[8192]{0:T(1024)S(1)} %dynamic-update-slice.1), channel_id=1, replica_groups=mesh['gx'=8,'gy'=32] {'gx','gy'}, use_global_device_ids=true, to_apply=%add.11 | all-reduce | flops 8192 | bytes 65536
  308.9 0.9 fusion.7
  309.8 2.0 fusion.132
  311.8 2.9 collective-permute-start.17
  314.8 1.9 collective-permute-start.16
  316.8 3.1 collective-permute-done.16
  319.9 1.3 collective-permute-start.18
  321.2 4.0 collective-permute-start.19
  325.2 0.8 collective-permute-done.19
  326.0 0.2 select_maximum_fusion.4
  326.4 3.1 collective-permute-start.20
  329.4 1.9 collective-permute-start.21
  331.4 3.3 collective-permute-done.21
  334.7 3.9 collective-permute-start.22
  338.6 1.3 collective-permute-start.23
  339.9 3.3 collective-permute-done.23
  343.3 0.4 add_multiply_fusion.1
  343.7 0.4 bitcast_multiply_fusion
  344.2 0.3 fusion.67
  344.4 1.1 fusion.80
  345.5 1.9 collective-permute-start.24
  347.4 3.6 collective-permute-start.25
  351.1 0.8 collective-permute-done.25
  352.0 1.3 collective-permute-start.26
  353.3 4.0 collective-permute-start.27
  357.3 0.8 collective-permute-done.27
  358.0 0.2 select_maximum_fusion
  358.3 0.7 multiply_reduce_fusion
  359.0 84.4 %all-reduce.12 = (f32[]{:T(128)}, f32[]{:T(128)}) all-reduce(f32[]{:T(128)} %get-tuple-element.3, f32[]{:T(128)} %get-tuple-element.2), channel_id=1, replica_groups=mesh['gx'=8,'gy'=32] {'gx','gy'}, use_global_device_ids=true, to_apply=%region_5.6 | all-reduce | flops 2 | bytes 16 | tf_op jit(solution)/shard_map/psum | solution.py:97
  444.8 0.7 multiply_subtract_fusion
  (77 shorter events, 2.2 us)
Async XLA Ops:
  0.6 86.7 %copy-start = (f32[32,8192]{1,0:T(8,128)S(1)}, f32[32,8192]{1,0:T(8,128)}, u32[]{:S(2)}) copy-start(f32[32,8192]{1,0:T(8,128)} %param.7) | copy-start | bytes 3145732
  0.6 85.5 %copy-start.3 = (bf16[32,8,16,256]{3,2,1,0:T(8,128)(2,1)S(1)}, bf16[32,8,16,256]{3,2,1,0:T(8,128)(2,1)}, u32[]{:S(2)}) copy-start(bf16[32,8,16,256]{3,2,1,0:T(8,128)(2,1)} %param.6) | copy-start | bytes 6291460
  86.1 1.2 copy-start.6
  87.3 1.4 copy-start.1
  87.3 6.1 %copy-start.2 = (f32[3,8,16,256]{3,2,1,0:T(8,128)S(1)}, f32[3,8,16,256]{3,2,1,0:T(8,128)}, u32[]{:S(2)}) copy-start(f32[3,8,16,256]{3,2,1,0:T(8,128)} %param.5) | copy-start | bytes 1179652
  88.3 16.8 %copy-start.4 = (f32[8,16,256]{2,1,0:T(8,128)S(1)}, f32[8,16,256]{2,1,0:T(8,128)}, u32[]{:S(2)}) copy-start(f32[8,16,256]{2,1,0:T(8,128)} %param.4) | copy-start | bytes 393220
  89.1 9.6 %collective-permute-start.5 = (f32[1,16,256]{2,1,0:T(8,128)S(1)}, f32[1,16,256]{2,1,0:T(8,128)S(1)}, u32[]{:S(2)}, u32[]{:S(2)}) collective-permute-start(f32[1,16,256]{2,1,0:T(8,128)S(1)} %slice.464), channel_id=1, source_target_pairs={{0,32},{32,64},{64,96},{96,128},{128,160},{160,192},{192,224},{1,3... | collective-permute-start | bytes 49160 | tf_op jit(solution)/shard_map/ppermute | solution.py:18
  91.0 7.7 %collective-permute-start.4 = (f32[1,16,256]{2,1,0:T(8,128)S(1)}, f32[1,16,256]{2,1,0:T(8,128)S(1)}, u32[]{:S(2)}, u32[]{:S(2)}) collective-permute-start(f32[1,16,256]{2,1,0:T(8,128)S(1)} %slice.461), channel_id=1, source_target_pairs={{32,0},{64,32},{96,64},{128,96},{160,128},{192,160},{224,192},{33,... | collective-permute-start | bytes 49160 | tf_op jit(solution)/shard_map/ppermute | solution.py:21
  93.5 18.5 %collective-permute-start = (f32[3,2,16,256]{3,2,1,0:T(8,128)S(1)}, f32[3,2,16,256]{3,2,1,0:T(8,128)S(1)}, u32[]{:S(2)}, u32[]{:S(2)}) collective-permute-start(f32[3,2,16,256]{3,2,1,0:T(8,128)S(1)} %get-tuple-element.31), channel_id=1, source_target_pairs={{0,32},{32,64},{64,96},{96,128},{128,160},{160,192},{192,224},{1,3... | collective-permute-start | bytes 294920 | tf_op jit(solution)/shard_map/ppermute | solution.py:18
  96.6 15.4 %collective-permute-start.1 = (f32[3,2,16,256]{3,2,1,0:T(8,128)S(1)}, f32[3,2,16,256]{3,2,1,0:T(8,128)S(1)}, u32[]{:S(2)}, u32[]{:S(2)}) collective-permute-start(f32[3,2,16,256]{3,2,1,0:T(8,128)S(1)} %get-tuple-element.30), channel_id=1, source_target_pairs={{32,0},{64,32},{96,64},{128,96},{160,128},{192,160},{224,192},{33,... | collective-permute-start | bytes 294920 | tf_op jit(solution)/shard_map/ppermute | solution.py:21
  98.7 5.4 %collective-permute-start.6 = (f32[10,1,256]{2,1,0:T(1,128)S(1)}, f32[10,1,256]{2,1,0:T(1,128)S(1)}, u32[]{:S(2)}, u32[]{:S(2)}) collective-permute-start(f32[10,1,256]{2,1,0:T(1,128)S(1)} %get-tuple-element.43), channel_id=1, source_target_pairs={{1,0},{2,1},{3,2},{4,3},{5,4},{6,5},{7,6},{8,7},{9,8},{10,9},{11,1... | collective-permute-start | bytes 30728 | tf_op jit(solution)/shard_map/ppermute | solution.py:21
  100.0 4.8 %collective-permute-start.7 = (f32[10,1,256]{2,1,0:T(1,128)S(1)}, f32[10,1,256]{2,1,0:T(1,128)S(1)}, u32[]{:S(2)}, u32[]{:S(2)}) collective-permute-start(f32[10,1,256]{2,1,0:T(1,128)S(1)} %get-tuple-element.42), channel_id=1, source_target_pairs={{0,1},{1,2},{2,3},{3,4},{4,5},{5,6},{6,7},{7,8},{8,9},{9,10},{10,1... | collective-permute-start | bytes 30728 | tf_op jit(solution)/shard_map/ppermute | solution.py:18
  105.2 12.1 %collective-permute-start.8 = (f32[2,16,256]{2,1,0:T(8,128)S(1)}, f32[2,16,256]{2,1,0:T(8,128)S(1)}, u32[]{:S(2)}, u32[]{:S(2)}) collective-permute-start(f32[2,16,256]{2,1,0:T(8,128)S(1)} %get-tuple-element.52), channel_id=1, source_target_pairs={{0,32},{32,64},{64,96},{96,128},{128,160},{160,192},{192,224},{1,3... | collective-permute-start | bytes 98312 | tf_op jit(solution)/shard_map/ppermute | solution.py:18
  110.0 7.3 %collective-permute-start.9 = (f32[2,16,256]{2,1,0:T(8,128)S(1)}, f32[2,16,256]{2,1,0:T(8,128)S(1)}, u32[]{:S(2)}, u32[]{:S(2)}) collective-permute-start(f32[2,16,256]{2,1,0:T(8,128)S(1)} %get-tuple-element.53), channel_id=1, source_target_pairs={{32,0},{64,32},{96,64},{128,96},{160,128},{192,160},{224,192},{33,... | collective-permute-start | bytes 98312 | tf_op jit(solution)/shard_map/ppermute | solution.py:21
  112.1 10.6 %collective-permute-start.2 = (f32[3,12,2,256]{3,2,1,0:T(2,128)S(1)}, f32[3,12,2,256]{3,2,1,0:T(2,128)S(1)}, u32[]{:S(2)}, u32[]{:S(2)}) collective-permute-start(f32[3,12,2,256]{3,2,1,0:T(2,128)S(1)} %get-tuple-element.28), channel_id=1, source_target_pairs={{0,1},{1,2},{2,3},{3,4},{4,5},{5,6},{6,7},{7,8},{8,9},{9,10},{10,1... | collective-permute-start | bytes 221192 | tf_op jit(solution)/shard_map/ppermute | solution.py:18
  116.0 6.7 %collective-permute-start.3 = (f32[3,12,2,256]{3,2,1,0:T(2,128)S(1)}, f32[3,12,2,256]{3,2,1,0:T(2,128)S(1)}, u32[]{:S(2)}, u32[]{:S(2)}) collective-permute-start(f32[3,12,2,256]{3,2,1,0:T(2,128)S(1)} %get-tuple-element.29), channel_id=1, source_target_pairs={{1,0},{2,1},{3,2},{4,3},{5,4},{6,5},{7,6},{8,7},{9,8},{10,9},{11,1... | collective-permute-start | bytes 221192 | tf_op jit(solution)/shard_map/ppermute | solution.py:21
  117.4 5.5 %collective-permute-start.10 = (f32[12,2,256]{2,1,0:T(2,128)S(1)}, f32[12,2,256]{2,1,0:T(2,128)S(1)}, u32[]{:S(2)}, u32[]{:S(2)}) collective-permute-start(f32[12,2,256]{2,1,0:T(2,128)S(1)} %get-tuple-element.34), channel_id=1, source_target_pairs={{0,1},{1,2},{2,3},{3,4},{4,5},{5,6},{6,7},{7,8},{8,9},{9,10},{10,1... | collective-permute-start | bytes 73736 | tf_op jit(solution)/shard_map/ppermute | solution.py:18
  121.4 4.6 %collective-permute-start.11 = (f32[12,2,256]{2,1,0:T(2,128)S(1)}, f32[12,2,256]{2,1,0:T(2,128)S(1)}, u32[]{:S(2)}, u32[]{:S(2)}) collective-permute-start(f32[12,2,256]{2,1,0:T(2,128)S(1)} %get-tuple-element.35), channel_id=1, source_target_pairs={{1,0},{2,1},{3,2},{4,3},{5,4},{6,5},{7,6},{8,7},{9,8},{10,9},{11,1... | collective-permute-start | bytes 73736 | tf_op jit(solution)/shard_map/ppermute | solution.py:21
  122.9 4.3 copy-start.5
  127.3 7.6 %collective-permute-start.12 = (f32[1,16,256]{2,1,0:T(8,128)S(1)}, f32[1,16,256]{2,1,0:T(8,128)S(1)}, u32[]{:S(2)}, u32[]{:S(2)}) collective-permute-start(f32[1,16,256]{2,1,0:T(8,128)S(1)} %get-tuple-element.51), channel_id=1, source_target_pairs={{32,0},{64,32},{96,64},{128,96},{160,128},{192,160},{224,192},{33,... | collective-permute-start | bytes 49160 | tf_op jit(solution)/shard_map/ppermute | solution.py:21
  129.3 6.5 %collective-permute-start.13 = (f32[1,16,256]{2,1,0:T(8,128)S(1)}, f32[1,16,256]{2,1,0:T(8,128)S(1)}, u32[]{:S(2)}, u32[]{:S(2)}) collective-permute-start(f32[1,16,256]{2,1,0:T(8,128)S(1)} %get-tuple-element.50), channel_id=1, source_target_pairs={{0,32},{32,64},{64,96},{96,128},{128,160},{160,192},{192,224},{1,3... | collective-permute-start | bytes 49160 | tf_op jit(solution)/shard_map/ppermute | solution.py:18
  135.8 5.3 %collective-permute-start.14 = (f32[10,1,256]{2,1,0:T(1,128)S(1)}, f32[10,1,256]{2,1,0:T(1,128)S(1)}, u32[]{:S(2)}, u32[]{:S(2)}) collective-permute-start(f32[10,1,256]{2,1,0:T(1,128)S(1)} %get-tuple-element.41), channel_id=1, source_target_pairs={{1,0},{2,1},{3,2},{4,3},{5,4},{6,5},{7,6},{8,7},{9,8},{10,9},{11,1... | collective-permute-start | bytes 30728 | tf_op jit(solution)/shard_map/ppermute | solution.py:21
  137.1 4.8 %collective-permute-start.15 = (f32[10,1,256]{2,1,0:T(1,128)S(1)}, f32[10,1,256]{2,1,0:T(1,128)S(1)}, u32[]{:S(2)}, u32[]{:S(2)}) collective-permute-start(f32[10,1,256]{2,1,0:T(1,128)S(1)} %get-tuple-element.40), channel_id=1, source_target_pairs={{0,1},{1,2},{2,3},{3,4},{4,5},{5,6},{6,7},{7,8},{8,9},{9,10},{10,1... | collective-permute-start | bytes 30728 | tf_op jit(solution)/shard_map/ppermute | solution.py:18
  311.8 4.9 %collective-permute-start.17 = (f32[1,16,256]{2,1,0:T(8,128)S(1)}, f32[1,16,256]{2,1,0:T(8,128)S(1)}, u32[]{:S(2)}, u32[]{:S(2)}) collective-permute-start(f32[1,16,256]{2,1,0:T(8,128)S(1)} %slice.509), channel_id=1, source_target_pairs={{0,32},{32,64},{64,96},{96,128},{128,160},{160,192},{192,224},{1,3... | collective-permute-start | bytes 49160 | tf_op jit(solution)/shard_map/ppermute | solution.py:18
  314.8 5.1 %collective-permute-start.16 = (f32[1,16,256]{2,1,0:T(8,128)S(1)}, f32[1,16,256]{2,1,0:T(8,128)S(1)}, u32[]{:S(2)}, u32[]{:S(2)}) collective-permute-start(f32[1,16,256]{2,1,0:T(8,128)S(1)} %slice.506), channel_id=1, source_target_pairs={{32,0},{64,32},{96,64},{128,96},{160,128},{192,160},{224,192},{33,... | collective-permute-start | bytes 49160 | tf_op jit(solution)/shard_map/ppermute | solution.py:21
  319.9 5.3 %collective-permute-start.18 = (f32[10,1,256]{2,1,0:T(1,128)S(1)}, f32[10,1,256]{2,1,0:T(1,128)S(1)}, u32[]{:S(2)}, u32[]{:S(2)}) collective-permute-start(f32[10,1,256]{2,1,0:T(1,128)S(1)} %get-tuple-element.39), channel_id=1, source_target_pairs={{1,0},{2,1},{3,2},{4,3},{5,4},{6,5},{7,6},{8,7},{9,8},{10,9},{11,1... | collective-permute-start | bytes 30728 | tf_op jit(solution)/shard_map/ppermute | solution.py:21
  321.2 4.8 %collective-permute-start.19 = (f32[10,1,256]{2,1,0:T(1,128)S(1)}, f32[10,1,256]{2,1,0:T(1,128)S(1)}, u32[]{:S(2)}, u32[]{:S(2)}) collective-permute-start(f32[10,1,256]{2,1,0:T(1,128)S(1)} %get-tuple-element.38), channel_id=1, source_target_pairs={{0,1},{1,2},{2,3},{3,4},{4,5},{5,6},{6,7},{7,8},{8,9},{9,10},{10,1... | collective-permute-start | bytes 30728 | tf_op jit(solution)/shard_map/ppermute | solution.py:18
  326.4 5.0 %collective-permute-start.20 = (f32[2,16,256]{2,1,0:T(8,128)S(1)}, f32[2,16,256]{2,1,0:T(8,128)S(1)}, u32[]{:S(2)}, u32[]{:S(2)}) collective-permute-start(f32[2,16,256]{2,1,0:T(8,128)S(1)} %get-tuple-element.46), channel_id=1, source_target_pairs={{0,32},{32,64},{64,96},{96,128},{128,160},{160,192},{192,224},{1,3... | collective-permute-start | bytes 98312 | tf_op jit(solution)/shard_map/ppermute | solution.py:18
  329.4 5.2 %collective-permute-start.21 = (f32[2,16,256]{2,1,0:T(8,128)S(1)}, f32[2,16,256]{2,1,0:T(8,128)S(1)}, u32[]{:S(2)}, u32[]{:S(2)}) collective-permute-start(f32[2,16,256]{2,1,0:T(8,128)S(1)} %get-tuple-element.47), channel_id=1, source_target_pairs={{32,0},{64,32},{96,64},{128,96},{160,128},{192,160},{224,192},{33,... | collective-permute-start | bytes 98312 | tf_op jit(solution)/shard_map/ppermute | solution.py:21
  334.7 5.2 %collective-permute-start.22 = (f32[12,2,256]{2,1,0:T(2,128)S(1)}, f32[12,2,256]{2,1,0:T(2,128)S(1)}, u32[]{:S(2)}, u32[]{:S(2)}) collective-permute-start(f32[12,2,256]{2,1,0:T(2,128)S(1)} %get-tuple-element.32), channel_id=1, source_target_pairs={{0,1},{1,2},{2,3},{3,4},{4,5},{5,6},{6,7},{7,8},{8,9},{9,10},{10,1... | collective-permute-start | bytes 73736 | tf_op jit(solution)/shard_map/ppermute | solution.py:18
  338.6 4.6 %collective-permute-start.23 = (f32[12,2,256]{2,1,0:T(2,128)S(1)}, f32[12,2,256]{2,1,0:T(2,128)S(1)}, u32[]{:S(2)}, u32[]{:S(2)}) collective-permute-start(f32[12,2,256]{2,1,0:T(2,128)S(1)} %get-tuple-element.33), channel_id=1, source_target_pairs={{1,0},{2,1},{3,2},{4,3},{5,4},{6,5},{7,6},{8,7},{9,8},{10,9},{11,1... | collective-permute-start | bytes 73736 | tf_op jit(solution)/shard_map/ppermute | solution.py:21
  345.5 5.6 %collective-permute-start.24 = (f32[1,16,256]{2,1,0:T(8,128)S(1)}, f32[1,16,256]{2,1,0:T(8,128)S(1)}, u32[]{:S(2)}, u32[]{:S(2)}) collective-permute-start(f32[1,16,256]{2,1,0:T(8,128)S(1)} %get-tuple-element.45), channel_id=1, source_target_pairs={{32,0},{64,32},{96,64},{128,96},{160,128},{192,160},{224,192},{33,... | collective-permute-start | bytes 49160 | tf_op jit(solution)/shard_map/ppermute | solution.py:21
  347.4 4.5 %collective-permute-start.25 = (f32[1,16,256]{2,1,0:T(8,128)S(1)}, f32[1,16,256]{2,1,0:T(8,128)S(1)}, u32[]{:S(2)}, u32[]{:S(2)}) collective-permute-start(f32[1,16,256]{2,1,0:T(8,128)S(1)} %get-tuple-element.44), channel_id=1, source_target_pairs={{0,32},{32,64},{64,96},{96,128},{128,160},{160,192},{192,224},{1,3... | collective-permute-start | bytes 49160 | tf_op jit(solution)/shard_map/ppermute | solution.py:18
  352.0 5.3 %collective-permute-start.26 = (f32[10,1,256]{2,1,0:T(1,128)S(1)}, f32[10,1,256]{2,1,0:T(1,128)S(1)}, u32[]{:S(2)}, u32[]{:S(2)}) collective-permute-start(f32[10,1,256]{2,1,0:T(1,128)S(1)} %get-tuple-element.37), channel_id=1, source_target_pairs={{1,0},{2,1},{3,2},{4,3},{5,4},{6,5},{7,6},{8,7},{9,8},{10,9},{11,1... | collective-permute-start | bytes 30728 | tf_op jit(solution)/shard_map/ppermute | solution.py:21
  353.3 4.8 %collective-permute-start.27 = (f32[10,1,256]{2,1,0:T(1,128)S(1)}, f32[10,1,256]{2,1,0:T(1,128)S(1)}, u32[]{:S(2)}, u32[]{:S(2)}) collective-permute-start(f32[10,1,256]{2,1,0:T(1,128)S(1)} %get-tuple-element.36), channel_id=1, source_target_pairs={{0,1},{1,2},{2,3},{3,4},{4,5},{5,6},{6,7},{7,8},{8,9},{9,10},{10,1... | collective-permute-start | bytes 30728 | tf_op jit(solution)/shard_map/ppermute | solution.py:18
where the time goes:
time: 447 us; the launch traced here: 446 us
  blocking collectives  327 us (73%)
  starting transfers between devices  75.8 us (17%)
  waiting for transfers between devices  17.4 us (4%)
  matrix products  10 us (2%)
  other arithmetic  8.6 us (2%)
    unnamed x2, blocking collectives  155 us
    psum x1, blocking collectives, local(): rho_now = lax.psum(jnp.sum(right_side * right_side), ('gx', 'gy'))  87.5 us
    psum x1, blocking collectives, local(): lax.psum((jnp.sum(turned * middle), jnp.sum(turned * turned)), ('gx', 'gy'))  84.4 us
    ppermute x14, starting transfers between devices, with_halo(): lax.ppermute(lax.slice_in_dim(block, block.shape[dim] - width, None, axis...  52.8 us
    ppermute x14, starting transfers between devices, with_halo(): lax.ppermute(lax.slice_in_dim(block, 0, width, axis=dim), axis, backward)  23 us
    ppermute x14, waiting for transfers between devices, with_halo(): lax.ppermute(lax.slice_in_dim(block, 0, width, axis=dim), axis, backward)  12.7 us
  transfers between devices with their start and end apart: 28, of which 10 were waited for; matrix products, arithmetic and copies ran while one was open for 0% of the time, Pallas kernels for 0%

commit v1 on v0

--- a/solution.py
+++ b/solution.py
@@ -94,7 +94,9 @@
     middle = right_side - alpha_step * image
     smoothed = precondition(middle, velocity, wide_velocity, flat_vectors, inverse_rows, inside)
     turned = apply_global(smoothed, velocity)
-    cross, square = lax.psum((jnp.sum(turned * middle), jnp.sum(turned * turned)), ("gx", "gy"))
+    cross, square = lax.psum(
+        lax.psum((jnp.sum(turned * middle), jnp.sum(turned * turned)), "gx"), "gy"
+    )
     omega_step = cross / square
     solution_field = alpha_step * search + omega_step * smoothed
     return (solution_field, middle - omega_step * turned)

time: 447 us -> 448 us (level)
  the two profiles are of different devices: /device:TPU:1 before, /device:TPU:8 now
where the time goes in v1:
time: 448 us; the launch traced here: 447 us
  blocking collectives  321 us (72%)
  starting transfers between devices  76.7 us (17%)
  waiting for transfers between devices  22.4 us (5%)
  matrix products  10 us (2%)
  other arithmetic  8.52 us (2%)
    unnamed x2, blocking collectives  153 us
    psum x1, blocking collectives, local(): rho_now = lax.psum(jnp.sum(right_side * right_side), ('gx', 'gy'))  83.9 us
    psum x1, blocking collectives, local(): lax.psum(lax.psum((jnp.sum(turned * middle), jnp.sum(turned * turned)), '...  73 us
    ppermute x14, starting transfers between devices, with_halo(): lax.ppermute(lax.slice_in_dim(block, block.shape[dim] - width, None, axis...  45.2 us
    ppermute x14, starting transfers between devices, with_halo(): lax.ppermute(lax.slice_in_dim(block, 0, width, axis=dim), axis, backward)  31.5 us
    ppermute x14, waiting for transfers between devices, with_halo(): lax.ppermute(lax.slice_in_dim(block, 0, width, axis=dim), axis, backward)  11.4 us
    ppermute x14, waiting for transfers between devices, with_halo(): lax.ppermute(lax.slice_in_dim(block, block.shape[dim] - width, None, axis...  11.1 us
    psum x1, blocking collectives, local(): lax.psum((jnp.sum(turned * middle), jnp.sum(turned * turned)), 'gx')  10.6 us
  transfers between devices with their start and end apart: 28, of which 11 were waited for; matrix products, arithmetic and copies ran while one was open for 0% of the time, Pallas kernels for 0%

profile of v1, /device:TPU:8, one launch (start us, length us, event | category | flops | bytes accessed | tf_op | source)
XLA Modules:
  0.0 446.6 jit_solution(7868631924875112714)
XLA Ops:
  0.7 1.0 convert_bitcast_fusion.1
  1.7 2.8 fusion.8
  4.7 78.6 %all-reduce.10 = f32[8192]{0:T(1024)S(1)} all-reduce(f32[8192]{0:T(1024)S(1)} %dynamic-update-slice), channel_id=1, replica_groups=mesh['gx'=8,'gy'=32] {'gx','gy'}, use_global_device_ids=true, to_apply=%add.10 | all-reduce | flops 8192 | bytes 65536
  83.4 2.8 copy.11
  86.2 0.9 fusion.5
  87.1 0.4 copy-done.1
  87.5 0.4 fusion.131
  87.9 1.9 collective-permute-start.5
  89.8 3.7 collective-permute-start.4
  93.6 1.9 collective-permute-start
  95.5 3.6 collective-permute-start.1
  99.4 1.3 collective-permute-start.6
  100.7 4.5 %collective-permute-start.7 = (f32[10,1,256]{2,1,0:T(1,128)S(1)}, f32[10,1,256]{2,1,0:T(1,128)S(1)}, u32[]{:S(2)}, u32[]{:S(2)}) collective-permute-start(f32[10,1,256]{2,1,0:T(1,128)S(1)} %get-tuple-element.44), channel_id=1, source_target_pairs={{0,1},{1,2},{2,3},{3,4},{4,5},{5,6},{6,7},{7,8},{8,9},{9,10},{10,1... | collective-permute-start | bytes 30728 | tf_op jit(solution)/shard_map/ppermute | solution.py:18
  105.4 1.2 collective-permute-done.7
  106.6 0.2 select_maximum_fusion.10
  107.0 1.9 collective-permute-start.8
  108.9 3.6 collective-permute-start.9
  112.7 4.2 collective-permute-start.2
  116.9 1.3 collective-permute-start.3
  118.3 4.5 %collective-permute-start.10 = (f32[12,2,256]{2,1,0:T(2,128)S(1)}, f32[12,2,256]{2,1,0:T(2,128)S(1)}, u32[]{:S(2)}, u32[]{:S(2)}) collective-permute-start(f32[12,2,256]{2,1,0:T(2,128)S(1)} %get-tuple-element.36), channel_id=1, source_target_pairs={{0,1},{1,2},{2,3},{3,4},{4,5},{5,6},{6,7},{7,8},{8,9},{9,10},{10,1... | collective-permute-start | bytes 73736 | tf_op jit(solution)/shard_map/ppermute | solution.py:18
  122.8 1.3 collective-permute-start.11
  124.4 4.2 collective-permute-done.11
  128.7 0.4 add_multiply_fusion.3
  129.1 0.4 bitcast_multiply_fusion.3
  129.5 0.3 fusion.39
  130.0 1.9 collective-permute-start.12
  131.9 2.4 collective-permute-start.13
  134.3 2.6 collective-permute-done.13
  137.0 1.3 collective-permute-start.14
  138.3 4.5 %collective-permute-start.15 = (f32[10,1,256]{2,1,0:T(1,128)S(1)}, f32[10,1,256]{2,1,0:T(1,128)S(1)}, u32[]{:S(2)}, u32[]{:S(2)}) collective-permute-start(f32[10,1,256]{2,1,0:T(1,128)S(1)} %get-tuple-element.42), channel_id=1, source_target_pairs={{0,1},{1,2},{2,3},{3,4},{4,5},{5,6},{6,7},{7,8},{8,9},{9,10},{10,1... | collective-permute-start | bytes 30728 | tf_op jit(solution)/shard_map/ppermute | solution.py:18
  142.8 1.4 collective-permute-done.15
  144.4 0.8 multiply_reduce_fusion.2
  145.2 83.9 %all-reduce.12 = (f32[]{:T(128)}, f32[]{:T(128)}) all-reduce(f32[]{:T(128)} %get-tuple-element.5, f32[]{:T(128)} %get-tuple-element.4), channel_id=1, replica_groups=mesh['gx'=8,'gy'=32] {'gx','gy'}, use_global_device_ids=true, to_apply=%region_1.0 | all-reduce | flops 2 | bytes 16 | tf_op jit(solution)/shard_map/psum | solution.py:89
  230.4 3.0 fusion.11
  233.7 74.5 %all-reduce.11 = f32[8192]{0:T(1024)S(1)} all-reduce(f32[8192]{0:T(1024)S(1)} %dynamic-update-slice.1), channel_id=1, replica_groups=mesh['gx'=8,'gy'=32] {'gx','gy'}, use_global_device_ids=true, to_apply=%add.11 | all-reduce | flops 8192 | bytes 65536
  308.2 0.9 fusion.7
  309.1 2.0 fusion.132
  311.1 1.9 collective-permute-start.17
  313.1 3.6 collective-permute-start.16
  316.8 1.4 collective-permute-done.16
  318.2 1.3 collective-permute-start.18
  319.5 4.5 %collective-permute-start.19 = (f32[10,1,256]{2,1,0:T(1,128)S(1)}, f32[10,1,256]{2,1,0:T(1,128)S(1)}, u32[]{:S(2)}, u32[]{:S(2)}) collective-permute-start(f32[10,1,256]{2,1,0:T(1,128)S(1)} %get-tuple-element.40), channel_id=1, source_target_pairs={{0,1},{1,2},{2,3},{3,4},{4,5},{5,6},{6,7},{7,8},{8,9},{9,10},{10,1... | collective-permute-start | bytes 30728 | tf_op jit(solution)/shard_map/ppermute | solution.py:18
  324.1 1.4 collective-permute-done.19
  325.8 1.9 collective-permute-start.20
  327.8 3.6 collective-permute-start.21
  331.4 1.6 collective-permute-done.21
  333.0 4.2 collective-permute-start.22
  337.2 1.3 collective-permute-start.23
  338.7 4.2 collective-permute-done.23
  343.1 0.4 add_multiply_fusion.1
  343.5 0.4 bitcast_multiply_fusion
  343.9 0.3 fusion.67
  344.2 1.1 fusion.80
  345.3 2.2 collective-permute-start.24
  347.5 2.1 collective-permute-start.25
  349.6 2.9 collective-permute-done.25
  352.6 1.3 collective-permute-start.26
  353.9 4.5 %collective-permute-start.27 = (f32[10,1,256]{2,1,0:T(1,128)S(1)}, f32[10,1,256]{2,1,0:T(1,128)S(1)}, u32[]{:S(2)}, u32[]{:S(2)}) collective-permute-start(f32[10,1,256]{2,1,0:T(1,128)S(1)} %get-tuple-element.38), channel_id=1, source_target_pairs={{0,1},{1,2},{2,3},{3,4},{4,5},{5,6},{6,7},{7,8},{8,9},{9,10},{10,1... | collective-permute-start | bytes 30728 | tf_op jit(solution)/shard_map/ppermute | solution.py:18
  358.4 1.4 collective-permute-done.27
  359.8 0.2 select_maximum_fusion
  360.0 0.7 multiply_reduce_fusion
  360.8 10.6 %all-reduce.14 = (f32[]{:T(128)}, f32[]{:T(128)}) all-reduce(f32[]{:T(128)} %get-tuple-element.3, f32[]{:T(128)} %get-tuple-element.2), channel_id=1, replica_groups=mesh['gx'=8,'gy'=32] {'gx'}, use_global_device_ids=true, to_apply=%region_5.6 | all-reduce | flops 2 | bytes 16 | tf_op jit(solution)/shard_map/psum | solution.py:98
  371.4 73.0 %all-reduce.13 = (f32[]{:T(128)}, f32[]{:T(128)}) all-reduce(f32[]{:T(128)} %get-tuple-element.10, f32[]{:T(128)} %get-tuple-element.11), channel_id=1, replica_groups=mesh['gx'=8,'gy'=32] {'gy'}, use_global_device_ids=true, to_apply=%region_6.7 | all-reduce | flops 2 | bytes 16 | tf_op jit(solution)/shard_map/psum | solution.py:97
  445.8 0.7 multiply_subtract_fusion
  (74 shorter events, 2.6 us)
Async XLA Ops:
  0.6 85.5 %copy-start = (f32[32,8192]{1,0:T(8,128)S(1)}, f32[32,8192]{1,0:T(8,128)}, u32[]{:S(2)}) copy-start(f32[32,8192]{1,0:T(8,128)} %param.7) | copy-start | bytes 3145732
  86.1 1.4 copy-start.1
  86.1 7.4 %copy-start.2 = (f32[3,8,16,256]{3,2,1,0:T(8,128)S(1)}, f32[3,8,16,256]{3,2,1,0:T(8,128)}, u32[]{:S(2)}) copy-start(f32[3,8,16,256]{3,2,1,0:T(8,128)} %param.5) | copy-start | bytes 1179652
  87.1 19.7 %copy-start.3 = (f32[8,16,256]{2,1,0:T(8,128)S(1)}, f32[8,16,256]{2,1,0:T(8,128)}, u32[]{:S(2)}) copy-start(f32[8,16,256]{2,1,0:T(8,128)} %param.4) | copy-start | bytes 393220
  87.9 11.4 %collective-permute-start.5 = (f32[1,16,256]{2,1,0:T(8,128)S(1)}, f32[1,16,256]{2,1,0:T(8,128)S(1)}, u32[]{:S(2)}, u32[]{:S(2)}) collective-permute-start(f32[1,16,256]{2,1,0:T(8,128)S(1)} %slice.464), channel_id=1, source_target_pairs={{0,32},{32,64},{64,96},{96,128},{128,160},{160,192},{192,224},{1,3... | collective-permute-start | bytes 49160 | tf_op jit(solution)/shard_map/ppermute | solution.py:18
  89.8 9.5 %collective-permute-start.4 = (f32[1,16,256]{2,1,0:T(8,128)S(1)}, f32[1,16,256]{2,1,0:T(8,128)S(1)}, u32[]{:S(2)}, u32[]{:S(2)}) collective-permute-start(f32[1,16,256]{2,1,0:T(8,128)S(1)} %slice.461), channel_id=1, source_target_pairs={{32,0},{64,32},{96,64},{128,96},{160,128},{192,160},{224,192},{33,... | collective-permute-start | bytes 49160 | tf_op jit(solution)/shard_map/ppermute | solution.py:21
  93.6 19.0 %collective-permute-start = (f32[3,2,16,256]{3,2,1,0:T(8,128)S(1)}, f32[3,2,16,256]{3,2,1,0:T(8,128)S(1)}, u32[]{:S(2)}, u32[]{:S(2)}) collective-permute-start(f32[3,2,16,256]{3,2,1,0:T(8,128)S(1)} %get-tuple-element.33), channel_id=1, source_target_pairs={{0,32},{32,64},{64,96},{96,128},{128,160},{160,192},{192,224},{1,3... | collective-permute-start | bytes 294920 | tf_op jit(solution)/shard_map/ppermute | solution.py:18
  95.5 17.1 %collective-permute-start.1 = (f32[3,2,16,256]{3,2,1,0:T(8,128)S(1)}, f32[3,2,16,256]{3,2,1,0:T(8,128)S(1)}, u32[]{:S(2)}, u32[]{:S(2)}) collective-permute-start(f32[3,2,16,256]{3,2,1,0:T(8,128)S(1)} %get-tuple-element.32), channel_id=1, source_target_pairs={{32,0},{64,32},{96,64},{128,96},{160,128},{192,160},{224,192},{33,... | collective-permute-start | bytes 294920 | tf_op jit(solution)/shard_map/ppermute | solution.py:21
  99.4 6.0 %collective-permute-start.6 = (f32[10,1,256]{2,1,0:T(1,128)S(1)}, f32[10,1,256]{2,1,0:T(1,128)S(1)}, u32[]{:S(2)}, u32[]{:S(2)}) collective-permute-start(f32[10,1,256]{2,1,0:T(1,128)S(1)} %get-tuple-element.45), channel_id=1, source_target_pairs={{1,0},{2,1},{3,2},{4,3},{5,4},{6,5},{7,6},{8,7},{9,8},{10,9},{11,1... | collective-permute-start | bytes 30728 | tf_op jit(solution)/shard_map/ppermute | solution.py:21
  100.7 5.9 %collective-permute-start.7 = (f32[10,1,256]{2,1,0:T(1,128)S(1)}, f32[10,1,256]{2,1,0:T(1,128)S(1)}, u32[]{:S(2)}, u32[]{:S(2)}) collective-permute-start(f32[10,1,256]{2,1,0:T(1,128)S(1)} %get-tuple-element.44), channel_id=1, source_target_pairs={{0,1},{1,2},{2,3},{3,4},{4,5},{5,6},{6,7},{7,8},{8,9},{9,10},{10,1... | collective-permute-start | bytes 30728 | tf_op jit(solution)/shard_map/ppermute | solution.py:18
  107.0 11.2 %collective-permute-start.8 = (f32[2,16,256]{2,1,0:T(8,128)S(1)}, f32[2,16,256]{2,1,0:T(8,128)S(1)}, u32[]{:S(2)}, u32[]{:S(2)}) collective-permute-start(f32[2,16,256]{2,1,0:T(8,128)S(1)} %get-tuple-element.54), channel_id=1, source_target_pairs={{0,32},{32,64},{64,96},{96,128},{128,160},{160,192},{192,224},{1,3... | collective-permute-start | bytes 98312 | tf_op jit(solution)/shard_map/ppermute | solution.py:18
  108.9 9.3 %collective-permute-start.9 = (f32[2,16,256]{2,1,0:T(8,128)S(1)}, f32[2,16,256]{2,1,0:T(8,128)S(1)}, u32[]{:S(2)}, u32[]{:S(2)}) collective-permute-start(f32[2,16,256]{2,1,0:T(8,128)S(1)} %get-tuple-element.55), channel_id=1, source_target_pairs={{32,0},{64,32},{96,64},{128,96},{160,128},{192,160},{224,192},{33,... | collective-permute-start | bytes 98312 | tf_op jit(solution)/shard_map/ppermute | solution.py:21
  112.7 11.4 %collective-permute-start.2 = (f32[3,12,2,256]{3,2,1,0:T(2,128)S(1)}, f32[3,12,2,256]{3,2,1,0:T(2,128)S(1)}, u32[]{:S(2)}, u32[]{:S(2)}) collective-permute-start(f32[3,12,2,256]{3,2,1,0:T(2,128)S(1)} %get-tuple-element.30), channel_id=1, source_target_pairs={{0,1},{1,2},{2,3},{3,4},{4,5},{5,6},{6,7},{7,8},{8,9},{9,10},{10,1... | collective-permute-start | bytes 221192 | tf_op jit(solution)/shard_map/ppermute | solution.py:18
  116.9 7.2 %collective-permute-start.3 = (f32[3,12,2,256]{3,2,1,0:T(2,128)S(1)}, f32[3,12,2,256]{3,2,1,0:T(2,128)S(1)}, u32[]{:S(2)}, u32[]{:S(2)}) collective-permute-start(f32[3,12,2,256]{3,2,1,0:T(2,128)S(1)} %get-tuple-element.31), channel_id=1, source_target_pairs={{1,0},{2,1},{3,2},{4,3},{5,4},{6,5},{7,6},{8,7},{9,8},{10,9},{11,1... | collective-permute-start | bytes 221192 | tf_op jit(solution)/shard_map/ppermute | solution.py:21
  118.3 6.1 %collective-permute-start.10 = (f32[12,2,256]{2,1,0:T(2,128)S(1)}, f32[12,2,256]{2,1,0:T(2,128)S(1)}, u32[]{:S(2)}, u32[]{:S(2)}) collective-permute-start(f32[12,2,256]{2,1,0:T(2,128)S(1)} %get-tuple-element.36), channel_id=1, source_target_pairs={{0,1},{1,2},{2,3},{3,4},{4,5},{5,6},{6,7},{7,8},{8,9},{9,10},{10,1... | collective-permute-start | bytes 73736 | tf_op jit(solution)/shard_map/ppermute | solution.py:18
  122.8 5.7 %collective-permute-start.11 = (f32[12,2,256]{2,1,0:T(2,128)S(1)}, f32[12,2,256]{2,1,0:T(2,128)S(1)}, u32[]{:S(2)}, u32[]{:S(2)}) collective-permute-start(f32[12,2,256]{2,1,0:T(2,128)S(1)} %get-tuple-element.37), channel_id=1, source_target_pairs={{1,0},{2,1},{3,2},{4,3},{5,4},{6,5},{7,6},{8,7},{9,8},{10,9},{11,1... | collective-permute-start | bytes 73736 | tf_op jit(solution)/shard_map/ppermute | solution.py:21
  124.4 5.4 %copy-start.4 = (f32[12,20,256]{2,1,0:T(8,128)}, f32[12,20,256]{2,1,0:T(8,128)S(1)}, u32[]{:S(2)}) copy-start(f32[12,20,256]{2,1,0:T(8,128)S(1)} %get-tuple-element.21) | copy-start | bytes 737284
  130.0 4.3 collective-permute-start.12
  131.9 5.1 %collective-permute-start.13 = (f32[1,16,256]{2,1,0:T(8,128)S(1)}, f32[1,16,256]{2,1,0:T(8,128)S(1)}, u32[]{:S(2)}, u32[]{:S(2)}) collective-permute-start(f32[1,16,256]{2,1,0:T(8,128)S(1)} %get-tuple-element.52), channel_id=1, source_target_pairs={{0,32},{32,64},{64,96},{96,128},{128,160},{160,192},{192,224},{1,3... | collective-permute-start | bytes 49160 | tf_op jit(solution)/shard_map/ppermute | solution.py:18
  137.0 5.9 %collective-permute-start.14 = (f32[10,1,256]{2,1,0:T(1,128)S(1)}, f32[10,1,256]{2,1,0:T(1,128)S(1)}, u32[]{:S(2)}, u32[]{:S(2)}) collective-permute-start(f32[10,1,256]{2,1,0:T(1,128)S(1)} %get-tuple-element.43), channel_id=1, source_target_pairs={{1,0},{2,1},{3,2},{4,3},{5,4},{6,5},{7,6},{8,7},{9,8},{10,9},{11,1... | collective-permute-start | bytes 30728 | tf_op jit(solution)/shard_map/ppermute | solution.py:21
  138.3 5.9 %collective-permute-start.15 = (f32[10,1,256]{2,1,0:T(1,128)S(1)}, f32[10,1,256]{2,1,0:T(1,128)S(1)}, u32[]{:S(2)}, u32[]{:S(2)}) collective-permute-start(f32[10,1,256]{2,1,0:T(1,128)S(1)} %get-tuple-element.42), channel_id=1, source_target_pairs={{0,1},{1,2},{2,3},{3,4},{4,5},{5,6},{6,7},{7,8},{8,9},{9,10},{10,1... | collective-permute-start | bytes 30728 | tf_op jit(solution)/shard_map/ppermute | solution.py:18
  311.1 5.6 %collective-permute-start.17 = (f32[1,16,256]{2,1,0:T(8,128)S(1)}, f32[1,16,256]{2,1,0:T(8,128)S(1)}, u32[]{:S(2)}, u32[]{:S(2)}) collective-permute-start(f32[1,16,256]{2,1,0:T(8,128)S(1)} %slice.509), channel_id=1, source_target_pairs={{0,32},{32,64},{64,96},{96,128},{128,160},{160,192},{192,224},{1,3... | collective-permute-start | bytes 49160 | tf_op jit(solution)/shard_map/ppermute | solution.py:18
  313.1 5.1 %collective-permute-start.16 = (f32[1,16,256]{2,1,0:T(8,128)S(1)}, f32[1,16,256]{2,1,0:T(8,128)S(1)}, u32[]{:S(2)}, u32[]{:S(2)}) collective-permute-start(f32[1,16,256]{2,1,0:T(8,128)S(1)} %slice.506), channel_id=1, source_target_pairs={{32,0},{64,32},{96,64},{128,96},{160,128},{192,160},{224,192},{33,... | collective-permute-start | bytes 49160 | tf_op jit(solution)/shard_map/ppermute | solution.py:21
  318.2 5.9 %collective-permute-start.18 = (f32[10,1,256]{2,1,0:T(1,128)S(1)}, f32[10,1,256]{2,1,0:T(1,128)S(1)}, u32[]{:S(2)}, u32[]{:S(2)}) collective-permute-start(f32[10,1,256]{2,1,0:T(1,128)S(1)} %get-tuple-element.41), channel_id=1, source_target_pairs={{1,0},{2,1},{3,2},{4,3},{5,4},{6,5},{7,6},{8,7},{9,8},{10,9},{11,1... | collective-permute-start | bytes 30728 | tf_op jit(solution)/shard_map/ppermute | solution.py:21
  319.5 5.9 %collective-permute-start.19 = (f32[10,1,256]{2,1,0:T(1,128)S(1)}, f32[10,1,256]{2,1,0:T(1,128)S(1)}, u32[]{:S(2)}, u32[]{:S(2)}) collective-permute-start(f32[10,1,256]{2,1,0:T(1,128)S(1)} %get-tuple-element.40), channel_id=1, source_target_pairs={{0,1},{1,2},{2,3},{3,4},{4,5},{5,6},{6,7},{7,8},{8,9},{9,10},{10,1... | collective-permute-start | bytes 30728 | tf_op jit(solution)/shard_map/ppermute | solution.py:18
  325.8 5.6 %collective-permute-start.20 = (f32[2,16,256]{2,1,0:T(8,128)S(1)}, f32[2,16,256]{2,1,0:T(8,128)S(1)}, u32[]{:S(2)}, u32[]{:S(2)}) collective-permute-start(f32[2,16,256]{2,1,0:T(8,128)S(1)} %get-tuple-element.48), channel_id=1, source_target_pairs={{0,32},{32,64},{64,96},{96,128},{128,160},{160,192},{192,224},{1,3... | collective-permute-start | bytes 98312 | tf_op jit(solution)/shard_map/ppermute | solution.py:18
  327.8 5.2 %collective-permute-start.21 = (f32[2,16,256]{2,1,0:T(8,128)S(1)}, f32[2,16,256]{2,1,0:T(8,128)S(1)}, u32[]{:S(2)}, u32[]{:S(2)}) collective-permute-start(f32[2,16,256]{2,1,0:T(8,128)S(1)} %get-tuple-element.49), channel_id=1, source_target_pairs={{32,0},{64,32},{96,64},{128,96},{160,128},{192,160},{224,192},{33,... | collective-permute-start | bytes 98312 | tf_op jit(solution)/shard_map/ppermute | solution.py:21
  333.0 5.7 %collective-permute-start.22 = (f32[12,2,256]{2,1,0:T(2,128)S(1)}, f32[12,2,256]{2,1,0:T(2,128)S(1)}, u32[]{:S(2)}, u32[]{:S(2)}) collective-permute-start(f32[12,2,256]{2,1,0:T(2,128)S(1)} %get-tuple-element.34), channel_id=1, source_target_pairs={{0,1},{1,2},{2,3},{3,4},{4,5},{5,6},{6,7},{7,8},{8,9},{9,10},{10,1... | collective-permute-start | bytes 73736 | tf_op jit(solution)/shard_map/ppermute | solution.py:18
  337.2 5.7 %collective-permute-start.23 = (f32[12,2,256]{2,1,0:T(2,128)S(1)}, f32[12,2,256]{2,1,0:T(2,128)S(1)}, u32[]{:S(2)}, u32[]{:S(2)}) collective-permute-start(f32[12,2,256]{2,1,0:T(2,128)S(1)} %get-tuple-element.35), channel_id=1, source_target_pairs={{1,0},{2,1},{3,2},{4,3},{5,4},{6,5},{7,6},{8,7},{9,8},{10,9},{11,1... | collective-permute-start | bytes 73736 | tf_op jit(solution)/shard_map/ppermute | solution.py:21
  345.3 4.3 collective-permute-start.24
  347.5 5.1 %collective-permute-start.25 = (f32[1,16,256]{2,1,0:T(8,128)S(1)}, f32[1,16,256]{2,1,0:T(8,128)S(1)}, u32[]{:S(2)}, u32[]{:S(2)}) collective-permute-start(f32[1,16,256]{2,1,0:T(8,128)S(1)} %get-tuple-element.46), channel_id=1, source_target_pairs={{0,32},{32,64},{64,96},{96,128},{128,160},{160,192},{192,224},{1,3... | collective-permute-start | bytes 49160 | tf_op jit(solution)/shard_map/ppermute | solution.py:18
  352.6 5.9 %collective-permute-start.26 = (f32[10,1,256]{2,1,0:T(1,128)S(1)}, f32[10,1,256]{2,1,0:T(1,128)S(1)}, u32[]{:S(2)}, u32[]{:S(2)}) collective-permute-start(f32[10,1,256]{2,1,0:T(1,128)S(1)} %get-tuple-element.39), channel_id=1, source_target_pairs={{1,0},{2,1},{3,2},{4,3},{5,4},{6,5},{7,6},{8,7},{9,8},{10,9},{11,1... | collective-permute-start | bytes 30728 | tf_op jit(solution)/shard_map/ppermute | solution.py:21
  353.9 5.9 %collective-permute-start.27 = (f32[10,1,256]{2,1,0:T(1,128)S(1)}, f32[10,1,256]{2,1,0:T(1,128)S(1)}, u32[]{:S(2)}, u32[]{:S(2)}) collective-permute-start(f32[10,1,256]{2,1,0:T(1,128)S(1)} %get-tuple-element.38), channel_id=1, source_target_pairs={{0,1},{1,2},{2,3},{3,4},{4,5},{5,6},{6,7},{7,8},{8,9},{9,10},{10,1... | collective-permute-start | bytes 30728 | tf_op jit(solution)/shard_map/ppermute | solution.py:18
